TPU v7x, 256 devices: a whole 4x4x8 slice. The times are simulated.
256 devices in a mesh: section: 8 (over y, core), ctx: 32 (over z, x).
Axes of the slice: x: 4, y: 4, z: 8, core: 2. Of those that a mesh axis runs over, the one named last changes fastest.
Arguments:
- features: bfloat16 [8, 8192, 1536], P('section', 'ctx'), may hold values from -6 to 6
- conv_weight: float32 [8, 3, 1536], P('section'), may hold values from -3.5 to 3.5
- residues: float32 [8, 32, 16], P('section'), may hold values from -1.5 to 1.5
- decay_rates: float32 [8, 32, 16], P('section'), may hold values from 6.1035156e-05 to 0.1
- skip_gain: float32 [8, 512], P('section'), may hold values from -6 to 6
Outputs:
- passed: bfloat16 [8, 8192, 512], P('section', 'ctx')
All inputs are finite; a program needn't handle non-finite values.
Results may differ from a plain program's by a relative error of at most 0.0014.
Values may be sent and summed in bfloat16 or wider, within the bound.
A program may use at most 64 MiB of HBM per device.

v0:
```python
from functools import partial
import math

import jax
import jax.numpy as jnp
from jax import lax
from jax.sharding import PartitionSpec as P

HIGHEST = lax.Precision.HIGHEST


def partner_2(shard, axis, bit):
    return lax.ppermute(shard, axis, [(i, i ^ 1 << bit) for i in range(lax.axis_size(axis))])


def shifted(shard, axis, by):
    count = lax.axis_size(axis)
    pairs = [(i, i + by) for i in range(count) if 0 <= i + by < count]
    return lax.ppermute(shard, axis, pairs)


def shifted_2(block, axis, distance):
    devices = range(lax.axis_size(axis))
    route = [((i - distance) % len(devices), i) for i in devices]
    return lax.ppermute(block, axis, route)


def dft_tables(length, direction):
    row_index = lax.broadcasted_iota(jnp.int32, (length, length), 0)
    col_index = lax.broadcasted_iota(jnp.int32, (length, length), 1)
    angles = (row_index * col_index % length).astype(jnp.float32) * (
        direction * 2.0 * math.pi / length
    )
    return (jnp.cos(angles), jnp.sin(angles))


def complex_apply(tables, real_part, imag_part):
    cosines, sines = tables
    matmul = partial(jnp.dot, precision=HIGHEST, preferred_element_type=jnp.float32)
    return (
        matmul(cosines, real_part) - matmul(sines, imag_part),
        matmul(cosines, imag_part) + matmul(sines, real_part),
    )


def rotate(real_part, imag_part, cosines, sines):
    return (real_part * cosines - imag_part * sines, real_part * sines + imag_part * cosines)


def forward_pairwise(gated_re, gated_im, filter_re, filter_im, positions):
    level_count = lax.axis_size("ctx").bit_length() - 1
    own_index = lax.axis_index("ctx")
    local_rows = gated_re.shape[0]
    pieces = (gated_re, gated_im, filter_re, filter_im)
    for level_number in range(level_count):
        bit_number = level_count - 1 - level_number
        partner = partner_2((pieces[0], pieces[1], pieces[2], pieces[3]), "ctx", bit_number)
        half_span = (1 << bit_number) * local_rows
        is_upper = own_index // (1 << bit_number) % 2 == 0
        angles = (positions % half_span).astype(jnp.float32) * (-math.pi / half_span)
        turn_cos = jnp.cos(angles)[:, None]
        turn_sin = jnp.sin(angles)[:, None]
        updated = []
        for offset in (0, 2):
            differ_re = partner[offset] - pieces[offset]
            differ_im = partner[offset + 1] - pieces[offset + 1]
            turned_re, turned_im = rotate(differ_re, differ_im, turn_cos, turn_sin)
            updated.append(jnp.where(is_upper, pieces[offset] + partner[offset], turned_re))
            updated.append(jnp.where(is_upper, pieces[offset + 1] + partner[offset + 1], turned_im))
        pieces = (updated[0], updated[1], updated[2], updated[3])
    local_tables = dft_tables(local_rows, -1.0)
    gated_spec = complex_apply(local_tables, pieces[0], pieces[1])
    filter_spec = complex_apply(local_tables, pieces[2], pieces[3])
    return (gated_spec[0], gated_spec[1], filter_spec[0], filter_spec[1])


def inverse_pairwise(spec_re, spec_im, positions):
    level_count = lax.axis_size("ctx").bit_length() - 1
    own_index = lax.axis_index("ctx")
    local_rows = spec_re.shape[0]
    wave_re, wave_im = complex_apply(dft_tables(local_rows, 1.0), spec_re, spec_im)
    wave_re = wave_re * (1.0 / local_rows)
    wave_im = wave_im * (1.0 / local_rows)
    for bit_number in range(level_count):
        half_span = (1 << bit_number) * local_rows
        is_upper = own_index // (1 << bit_number) % 2 == 0
        angles = (positions % half_span).astype(jnp.float32) * (-math.pi / half_span)
        turn_cos = jnp.cos(angles)[:, None]
        turn_sin = jnp.sin(angles)[:, None]
        turned_re, turned_im = rotate(wave_re, wave_im, turn_cos, -turn_sin)
        sent_re = jnp.where(is_upper, wave_re, turned_re)
        sent_im = jnp.where(is_upper, wave_im, turned_im)
        other_re, other_im = partner_2((sent_re, sent_im), "ctx", bit_number)
        wave_re = jnp.where(is_upper, sent_re + other_re, other_re - sent_re) * 0.5
        wave_im = jnp.where(is_upper, sent_im + other_im, other_im - sent_im) * 0.5
    return (wave_re, wave_im)


def spectral_convolve(gated_input, residues_now, decay_now, positions, total_rows):
    local_rows, channels = gated_input.shape
    groups = residues_now.shape[0]
    time_index = positions.astype(jnp.float32)
    scaled = residues_now * jnp.sqrt(-jnp.expm1(-2.0 * decay_now))
    envelope = jnp.exp(-decay_now[None, :, :] * time_index[:, None, None])
    filter_time = jnp.einsum("gm,tgm->tg", scaled, envelope, precision=HIGHEST)
    theta = time_index * (math.pi / total_rows)
    shift_cos = jnp.cos(theta)[:, None]
    shift_sin = jnp.sin(theta)[:, None]
    gated_re = jnp.concatenate([gated_input, gated_input * shift_cos], axis=1)
    gated_im = jnp.concatenate([jnp.zeros_like(gated_input), -gated_input * shift_sin], axis=1)
    filter_re = jnp.concatenate([filter_time, filter_time * shift_cos], axis=1)
    filter_im = jnp.concatenate([jnp.zeros_like(filter_time), -filter_time * shift_sin], axis=1)
    spectra = forward_pairwise(gated_re, gated_im, filter_re, filter_im, positions)
    group_cols = spectra[0].shape[1] // (2 * groups)
    signal_re = spectra[0].reshape(local_rows, 2, groups, group_cols)
    signal_im = spectra[1].reshape(local_rows, 2, groups, group_cols)
    kernel_re = spectra[2].reshape(local_rows, 2, groups, 1)
    kernel_im = spectra[3].reshape(local_rows, 2, groups, 1)
    product_re = (signal_re * kernel_re - signal_im * kernel_im).reshape(
        local_rows, 2 * groups * group_cols
    )
    product_im = (signal_re * kernel_im + signal_im * kernel_re).reshape(
        local_rows, 2 * groups * group_cols
    )
    wave_re, wave_im = inverse_pairwise(product_re, product_im, positions)
    return 0.5 * (
        wave_re[:, :channels]
        + shift_cos * wave_re[:, channels:]
        - shift_sin * wave_im[:, channels:]
    )


def on_device(features, conv_weight, residues, decay_rates, skip_gain):
    local_rows = features.shape[1]
    device_count = lax.axis_size("ctx")
    own_index = lax.axis_index("ctx")
    total_rows = local_rows * device_count
    channels = skip_gain.shape[1]
    tap_count = conv_weight.shape[1]
    current = features[0]
    rim_rows = current[local_rows - (tap_count - 1) :]
    before = shifted(rim_rows, "ctx", 1)
    extended = jnp.concatenate([before, current], axis=0).astype(jnp.float32)
    shortened = jnp.zeros((local_rows, current.shape[1]), jnp.float32)
    for tap_index in range(tap_count):
        begin_row = tap_count - 1 - tap_index
        shortened = (
            shortened
            + conv_weight[0, tap_index][None, :] * extended[begin_row : begin_row + local_rows]
        )
    query_part = shortened[:, :channels]
    gated_input = shortened[:, channels : 2 * channels] * shortened[:, 2 * channels :]
    positions = own_index * local_rows + lax.broadcasted_iota(jnp.int32, (local_rows,), 0)
    convolved = spectral_convolve(gated_input, residues[0], decay_rates[0], positions, total_rows)
    mixer_sum = convolved + skip_gain[0][None, :] * gated_input
    section_output = (query_part * mixer_sum).astype(jnp.bfloat16)
    passed = shifted_2(section_output, "section", 1)
    return passed[None]


def solution(mesh):
    placed = (
        P("section", "ctx", None),
        P("section", None, None),
        P("section", None, None),
        P("section", None, None),
        P("section", None),
    )
    return jax.shard_map(
        on_device, mesh=mesh, in_specs=placed, out_specs=P("section", "ctx", None), check_vma=False
    )
```

profile of v0, /device:TPU:2, one launch (start us, length us, event | category | flops | bytes accessed | tf_op | source)
XLA Modules:
  0.0 729.4 jit_solution(14052327755012598)
XLA Ops:
  0.8 3.4 collective-permute-start
  9.4 7.2 collective-permute-start.1
  17.8 30.8 %collective-permute-done.1 = f32[256,1024]{1,0:T(8,128)} collective-permute-done((f32[256,1024]{1,0:T(8,128)}, f32[256,1024]{1,0:T(8,128)}, u32[]{:S(2)}, u32[]{:S(2)}) %collective-permute-start.1) | collective-permute-done | bytes 1048608 | tf_op jit(solution)/shard_map/ppermute | solution.py:13
  48.6 56.8 %collective-permute-done.2 = f32[256,1024]{1,0:T(8,128)} collective-permute-done((f32[256,1024]{1,0:T(8,128)}, f32[256,1024]{1,0:T(8,128)}, u32[]{:S(2)}, u32[]{:S(2)}) %collective-permute-start.2) | collective-permute-done | bytes 1048608 | tf_op jit(solution)/shard_map/ppermute | solution.py:13
  105.4 3.5 add_select_fusion.9
  108.8 2.9 collective-permute-start.3
  111.8 68.1 %collective-permute-done.3 = f32[256,1024]{1,0:T(8,128)S(1)} collective-permute-done((f32[256,1024]{1,0:T(8,128)}, f32[256,1024]{1,0:T(8,128)S(1)}, u32[]{:S(2)}, u32[]{:S(2)}) %collective-permute-start.3) | collective-permute-done | bytes 1048608 | tf_op jit(solution)/shard_map/ppermute | solution.py:13
  180.0 22.0 %collective-permute-done.4 = f32[256,1024]{1,0:T(8,128)} collective-permute-done((f32[256,1024]{1,0:T(8,128)}, f32[256,1024]{1,0:T(8,128)}, u32[]{:S(2)}, u32[]{:S(2)}) %collective-permute-start.4) | collective-permute-done | bytes 1048608 | tf_op jit(solution)/shard_map/ppermute | solution.py:13
  201.9 3.7 add_select_fusion.8
  209.1 4.6 collective-permute-start.11
  215.9 48.9 %collective-permute-done.11 = f32[256,64]{1,0:T(8,128)} collective-permute-done((f32[256,64]{1,0:T(8,128)}, f32[256,64]{1,0:T(8,128)}, u32[]{:S(2)}, u32[]{:S(2)}) %collective-permute-start.11) | collective-permute-done | bytes 65568 | tf_op jit(solution)/shard_map/ppermute | solution.py:13
  267.5 2.9 collective-permute-start.14
  272.8 4.6 collective-permute-start.7
  282.5 3.8 collective-permute-done.15
  287.8 7.5 %collective-permute-start.17 = (f32[256,64]{1,0:T(8,128)S(1)}, f32[256,64]{1,0:T(8,128)S(1)}, u32[]{:S(2)}, u32[]{:S(2)}) collective-permute-start(f32[256,64]{1,0:T(8,128)S(1)} %get-tuple-element.36), channel_id=1, source_target_pairs={{0,2},{1,3},{2,0},{3,1},{4,6},{5,7},{6,4},{7,5},{8,10},{9,11},{10,... | collective-permute-start | bytes 196616 | tf_op jit(solution)/shard_map/ppermute | solution.py:13
  295.4 30.9 %collective-permute-done.17 = f32[256,64]{1,0:T(8,128)S(1)} collective-permute-done((f32[256,64]{1,0:T(8,128)S(1)}, f32[256,64]{1,0:T(8,128)S(1)}, u32[]{:S(2)}, u32[]{:S(2)}) %collective-permute-start.17) | collective-permute-done | bytes 65568 | tf_op jit(solution)/shard_map/ppermute | solution.py:13
  348.7 10.8 %collective-permute-done.10 = f32[256,1024]{1,0:T(8,128)} collective-permute-done((f32[256,1024]{1,0:T(8,128)}, f32[256,1024]{1,0:T(8,128)}, u32[]{:S(2)}, u32[]{:S(2)}) %collective-permute-start.10) | collective-permute-done | bytes 1048608 | tf_op jit(solution)/shard_map/ppermute | solution.py:13
  359.5 20.1 %collective-permute-done.9 = f32[256,1024]{1,0:T(8,128)} collective-permute-done((f32[256,1024]{1,0:T(8,128)}, f32[256,1024]{1,0:T(8,128)}, u32[]{:S(2)}, u32[]{:S(2)}) %collective-permute-start.9) | collective-permute-done | bytes 1048608 | tf_op jit(solution)/shard_map/ppermute | solution.py:13
  402.1 23.8 %collective-permute-done.21 = f32[256,1024]{1,0:T(8,128)S(1)} collective-permute-done((f32[256,1024]{1,0:T(8,128)S(1)}, f32[256,1024]{1,0:T(8,128)S(1)}, u32[]{:S(2)}, u32[]{:S(2)}) %collective-permute-start.21) | collective-permute-done | bytes 1048608 | tf_op jit(solution)/shard_map/ppermute | solution.py:13
  425.9 19.3 %collective-permute-done.22 = f32[256,1024]{1,0:T(8,128)S(1)} collective-permute-done((f32[256,1024]{1,0:T(8,128)S(1)}, f32[256,1024]{1,0:T(8,128)S(1)}, u32[]{:S(2)}, u32[]{:S(2)}) %collective-permute-start.22) | collective-permute-done | bytes 1048608 | tf_op jit(solution)/shard_map/ppermute | solution.py:13
  445.9 3.7 collective-permute-start.23
  449.8 23.9 %collective-permute-done.23 = f32[256,1024]{1,0:T(8,128)S(1)} collective-permute-done((f32[256,1024]{1,0:T(8,128)S(1)}, f32[256,1024]{1,0:T(8,128)S(1)}, u32[]{:S(2)}, u32[]{:S(2)}) %collective-permute-start.23) | collective-permute-done | bytes 1048608 | tf_op jit(solution)/shard_map/ppermute | solution.py:13
  473.7 18.3 %collective-permute-done.24 = f32[256,1024]{1,0:T(8,128)S(1)} collective-permute-done((f32[256,1024]{1,0:T(8,128)S(1)}, f32[256,1024]{1,0:T(8,128)S(1)}, u32[]{:S(2)}, u32[]{:S(2)}) %collective-permute-start.24) | collective-permute-done | bytes 1048608 | tf_op jit(solution)/shard_map/ppermute | solution.py:13
  494.8 24.0 %collective-permute-done.25 = f32[256,1024]{1,0:T(8,128)S(1)} collective-permute-done((f32[256,1024]{1,0:T(8,128)S(1)}, f32[256,1024]{1,0:T(8,128)S(1)}, u32[]{:S(2)}, u32[]{:S(2)}) %collective-permute-start.25) | collective-permute-done | bytes 1048608 | tf_op jit(solution)/shard_map/ppermute | solution.py:13
  518.8 18.5 %collective-permute-done.26 = f32[256,1024]{1,0:T(8,128)S(1)} collective-permute-done((f32[256,1024]{1,0:T(8,128)S(1)}, f32[256,1024]{1,0:T(8,128)S(1)}, u32[]{:S(2)}, u32[]{:S(2)}) %collective-permute-start.26) | collective-permute-done | bytes 1048608 | tf_op jit(solution)/shard_map/ppermute | solution.py:13
  538.0 3.1 collective-permute-start.27
  541.3 64.1 %collective-permute-done.27 = f32[256,1024]{1,0:T(8,128)S(1)} collective-permute-done((f32[256,1024]{1,0:T(8,128)S(1)}, f32[256,1024]{1,0:T(8,128)S(1)}, u32[]{:S(2)}, u32[]{:S(2)}) %collective-permute-start.27) | collective-permute-done | bytes 1048608 | tf_op jit(solution)/shard_map/ppermute | solution.py:13
  605.4 20.0 %collective-permute-done.28 = f32[256,1024]{1,0:T(8,128)S(1)} collective-permute-done((f32[256,1024]{1,0:T(8,128)S(1)}, f32[256,1024]{1,0:T(8,128)S(1)}, u32[]{:S(2)}, u32[]{:S(2)}) %collective-permute-start.28) | collective-permute-done | bytes 1048608 | tf_op jit(solution)/shard_map/ppermute | solution.py:13
  626.0 3.7 collective-permute-start.29
  632.1 59.0 %collective-permute-done.29 = f32[256,1024]{1,0:T(8,128)S(1)} collective-permute-done((f32[256,1024]{1,0:T(8,128)S(1)}, f32[256,1024]{1,0:T(8,128)S(1)}, u32[]{:S(2)}, u32[]{:S(2)}) %collective-permute-start.29) | collective-permute-done | bytes 1048608 | tf_op jit(solution)/shard_map/ppermute | solution.py:13
  691.3 29.7 %collective-permute-done.30 = f32[256,1024]{1,0:T(8,128)S(1)} collective-permute-done((f32[256,1024]{1,0:T(8,128)S(1)}, f32[256,1024]{1,0:T(8,128)S(1)}, u32[]{:S(2)}, u32[]{:S(2)}) %collective-permute-start.30) | collective-permute-done | bytes 1048608 | tf_op jit(solution)/shard_map/ppermute | solution.py:13
  721.3 7.0 collective-permute-done.31
  (108 shorter events, 78.0 us)
Async XLA Ops:
  0.8 5.5 collective-permute-start
  9.4 39.2 %collective-permute-start.1 = (f32[256,1024]{1,0:T(8,128)}, f32[256,1024]{1,0:T(8,128)}, u32[]{:S(2)}, u32[]{:S(2)}) collective-permute-start(f32[256,1024]{1,0:T(8,128)} %pad_maximum_fusion), channel_id=1, source_target_pairs={{0,16},{1,17},{2,18},{3,19},{4,20},{5,21},{6,22},{7,23},{8,24},{9,... | collective-permute-start | bytes 3145736 | tf_op jit(solution)/shard_map/ppermute | solution.py:13
  17.7 87.7 %collective-permute-start.2 = (f32[256,1024]{1,0:T(8,128)}, f32[256,1024]{1,0:T(8,128)}, u32[]{:S(2)}, u32[]{:S(2)}) collective-permute-start(f32[256,1024]{1,0:T(8,128)} %concatenate.17), channel_id=1, source_target_pairs={{0,16},{1,17},{2,18},{3,19},{4,20},{5,21},{6,22},{7,23},{8,24},{9,... | collective-permute-start | bytes 3145736 | tf_op jit(solution)/shard_map/ppermute | solution.py:13
  108.8 71.1 %collective-permute-start.3 = (f32[256,1024]{1,0:T(8,128)}, f32[256,1024]{1,0:T(8,128)S(1)}, u32[]{:S(2)}, u32[]{:S(2)}) collective-permute-start(f32[256,1024]{1,0:T(8,128)} %get-tuple-element.29), channel_id=1, source_target_pairs={{0,8},{1,9},{2,10},{3,11},{4,12},{5,13},{6,14},{7,15},{8,0},{9,1},... | collective-permute-start | bytes 3145736 | tf_op jit(solution)/shard_map/ppermute | solution.py:13
  111.7 90.2 %collective-permute-start.4 = (f32[256,1024]{1,0:T(8,128)}, f32[256,1024]{1,0:T(8,128)}, u32[]{:S(2)}, u32[]{:S(2)}) collective-permute-start(f32[256,1024]{1,0:T(8,128)} %get-tuple-element.28), channel_id=1, source_target_pairs={{0,8},{1,9},{2,10},{3,11},{4,12},{5,13},{6,14},{7,15},{8,0},{9,1},... | collective-permute-start | bytes 3145736 | tf_op jit(solution)/shard_map/ppermute | solution.py:13
  205.7 64.7 %collective-permute-start.5 = (f32[256,1024]{1,0:T(8,128)}, f32[256,1024]{1,0:T(8,128)}, u32[]{:S(2)}, u32[]{:S(2)}) collective-permute-start(f32[256,1024]{1,0:T(8,128)} %get-tuple-element.25), channel_id=1, source_target_pairs={{0,4},{1,5},{2,6},{3,7},{4,0},{5,1},{6,2},{7,3},{8,12},{9,13},{10,... | collective-permute-start | bytes 3145736 | tf_op jit(solution)/shard_map/ppermute | solution.py:13
  205.7 64.7 %collective-permute-start.6 = (f32[256,1024]{1,0:T(8,128)S(1)}, f32[256,1024]{1,0:T(8,128)}, u32[]{:S(2)}, u32[]{:S(2)}) collective-permute-start(f32[256,1024]{1,0:T(8,128)S(1)} %get-tuple-element.24), channel_id=1, source_target_pairs={{0,4},{1,5},{2,6},{3,7},{4,0},{5,1},{6,2},{7,3},{8,12},{9,13},{10,... | collective-permute-start | bytes 3145736 | tf_op jit(solution)/shard_map/ppermute | solution.py:13
  209.1 55.7 %collective-permute-start.11 = (f32[256,64]{1,0:T(8,128)}, f32[256,64]{1,0:T(8,128)}, u32[]{:S(2)}, u32[]{:S(2)}) collective-permute-start(f32[256,64]{1,0:T(8,128)} %pad_maximum_fusion.1), channel_id=1, source_target_pairs={{0,16},{1,17},{2,18},{3,19},{4,20},{5,21},{6,22},{7,23},{8,24},{9,... | collective-permute-start | bytes 196616 | tf_op jit(solution)/shard_map/ppermute | solution.py:13
  214.5 51.7 %collective-permute-start.12 = (f32[256,64]{1,0:T(8,128)}, f32[256,64]{1,0:T(8,128)}, u32[]{:S(2)}, u32[]{:S(2)}) collective-permute-start(f32[256,64]{1,0:T(8,128)} %concatenate.19), channel_id=1, source_target_pairs={{0,16},{1,17},{2,18},{3,19},{4,20},{5,21},{6,22},{7,23},{8,24},{9,... | collective-permute-start | bytes 196616 | tf_op jit(solution)/shard_map/ppermute | solution.py:13
  267.4 11.0 %collective-permute-start.13 = (f32[256,64]{1,0:T(8,128)S(1)}, f32[256,64]{1,0:T(8,128)S(1)}, u32[]{:S(2)}, u32[]{:S(2)}) collective-permute-start(f32[256,64]{1,0:T(8,128)S(1)} %get-tuple-element.40), channel_id=1, source_target_pairs={{0,8},{1,9},{2,10},{3,11},{4,12},{5,13},{6,14},{7,15},{8,0},{9,1},... | collective-permute-start | bytes 196616 | tf_op jit(solution)/shard_map/ppermute | solution.py:13
  267.5 12.7 %collective-permute-start.14 = (f32[256,64]{1,0:T(8,128)S(1)}, f32[256,64]{1,0:T(8,128)S(1)}, u32[]{:S(2)}, u32[]{:S(2)}) collective-permute-start(f32[256,64]{1,0:T(8,128)S(1)} %get-tuple-element.41), channel_id=1, source_target_pairs={{0,8},{1,9},{2,10},{3,11},{4,12},{5,13},{6,14},{7,15},{8,0},{9,1},... | collective-permute-start | bytes 196616 | tf_op jit(solution)/shard_map/ppermute | solution.py:13
  272.8 57.5 %collective-permute-start.7 = (f32[256,1024]{1,0:T(8,128)S(1)}, f32[256,1024]{1,0:T(8,128)S(1)}, u32[]{:S(2)}, u32[]{:S(2)}) collective-permute-start(f32[256,1024]{1,0:T(8,128)S(1)} %get-tuple-element.23), channel_id=1, source_target_pairs={{0,2},{1,3},{2,0},{3,1},{4,6},{5,7},{6,4},{7,5},{8,10},{9,11},{10,... | collective-permute-start | bytes 3145736 | tf_op jit(solution)/shard_map/ppermute | solution.py:13
  277.4 52.9 %collective-permute-start.8 = (f32[256,1024]{1,0:T(8,128)S(1)}, f32[256,1024]{1,0:T(8,128)S(1)}, u32[]{:S(2)}, u32[]{:S(2)}) collective-permute-start(f32[256,1024]{1,0:T(8,128)S(1)} %get-tuple-element.22), channel_id=1, source_target_pairs={{0,2},{1,3},{2,0},{3,1},{4,6},{5,7},{6,4},{7,5},{8,10},{9,11},{10,... | collective-permute-start | bytes 3145736 | tf_op jit(solution)/shard_map/ppermute | solution.py:13
  280.3 5.9 collective-permute-start.15
  280.4 7.2 collective-permute-start.16
  287.8 38.5 %collective-permute-start.17 = (f32[256,64]{1,0:T(8,128)S(1)}, f32[256,64]{1,0:T(8,128)S(1)}, u32[]{:S(2)}, u32[]{:S(2)}) collective-permute-start(f32[256,64]{1,0:T(8,128)S(1)} %get-tuple-element.36), channel_id=1, source_target_pairs={{0,2},{1,3},{2,0},{3,1},{4,6},{5,7},{6,4},{7,5},{8,10},{9,11},{10,... | collective-permute-start | bytes 196616 | tf_op jit(solution)/shard_map/ppermute | solution.py:13
  295.3 32.4 %collective-permute-start.18 = (f32[256,64]{1,0:T(8,128)S(1)}, f32[256,64]{1,0:T(8,128)S(1)}, u32[]{:S(2)}, u32[]{:S(2)}) collective-permute-start(f32[256,64]{1,0:T(8,128)S(1)} %get-tuple-element.37), channel_id=1, source_target_pairs={{0,2},{1,3},{2,0},{3,1},{4,6},{5,7},{6,4},{7,5},{8,10},{9,11},{10,... | collective-permute-start | bytes 196616 | tf_op jit(solution)/shard_map/ppermute | solution.py:13
  327.9 6.5 collective-permute-start.19
  330.2 6.7 collective-permute-start.20
  332.2 27.3 %collective-permute-start.10 = (f32[256,1024]{1,0:T(8,128)}, f32[256,1024]{1,0:T(8,128)}, u32[]{:S(2)}, u32[]{:S(2)}) collective-permute-start(f32[256,1024]{1,0:T(8,128)} %get-tuple-element.20), channel_id=1, source_target_pairs={{0,1},{1,0},{2,3},{3,2},{4,5},{5,4},{6,7},{7,6},{8,9},{9,8},{10,11... | collective-permute-start | bytes 3145736 | tf_op jit(solution)/shard_map/ppermute | solution.py:13
  334.1 45.5 %collective-permute-start.9 = (f32[256,1024]{1,0:T(8,128)}, f32[256,1024]{1,0:T(8,128)}, u32[]{:S(2)}, u32[]{:S(2)}) collective-permute-start(f32[256,1024]{1,0:T(8,128)} %get-tuple-element.21), channel_id=1, source_target_pairs={{0,1},{1,0},{2,3},{3,2},{4,5},{5,4},{6,7},{7,6},{8,9},{9,8},{10,11... | collective-permute-start | bytes 3145736 | tf_op jit(solution)/shard_map/ppermute | solution.py:13
  399.7 26.2 %collective-permute-start.21 = (f32[256,1024]{1,0:T(8,128)S(1)}, f32[256,1024]{1,0:T(8,128)S(1)}, u32[]{:S(2)}, u32[]{:S(2)}) collective-permute-start(f32[256,1024]{1,0:T(8,128)S(1)} %get-tuple-element.31), channel_id=1, source_target_pairs={{0,1},{1,0},{2,3},{3,2},{4,5},{5,4},{6,7},{7,6},{8,9},{9,8},{10,11... | collective-permute-start | bytes 3145736 | tf_op jit(solution)/shard_map/ppermute | solution.py:13
  401.7 43.5 %collective-permute-start.22 = (f32[256,1024]{1,0:T(8,128)S(1)}, f32[256,1024]{1,0:T(8,128)S(1)}, u32[]{:S(2)}, u32[]{:S(2)}) collective-permute-start(f32[256,1024]{1,0:T(8,128)S(1)} %get-tuple-element.30), channel_id=1, source_target_pairs={{0,1},{1,0},{2,3},{3,2},{4,5},{5,4},{6,7},{7,6},{8,9},{9,8},{10,11... | collective-permute-start | bytes 3145736 | tf_op jit(solution)/shard_map/ppermute | solution.py:13
  445.9 27.8 %collective-permute-start.23 = (f32[256,1024]{1,0:T(8,128)S(1)}, f32[256,1024]{1,0:T(8,128)S(1)}, u32[]{:S(2)}, u32[]{:S(2)}) collective-permute-start(f32[256,1024]{1,0:T(8,128)S(1)} %get-tuple-element.17), channel_id=1, source_target_pairs={{0,2},{1,3},{2,0},{3,1},{4,6},{5,7},{6,4},{7,5},{8,10},{9,11},{10,... | collective-permute-start | bytes 3145736 | tf_op jit(solution)/shard_map/ppermute | solution.py:13
  449.6 42.4 %collective-permute-start.24 = (f32[256,1024]{1,0:T(8,128)S(1)}, f32[256,1024]{1,0:T(8,128)S(1)}, u32[]{:S(2)}, u32[]{:S(2)}) collective-permute-start(f32[256,1024]{1,0:T(8,128)S(1)} %get-tuple-element.16), channel_id=1, source_target_pairs={{0,2},{1,3},{2,0},{3,1},{4,6},{5,7},{6,4},{7,5},{8,10},{9,11},{10,... | collective-permute-start | bytes 3145736 | tf_op jit(solution)/shard_map/ppermute | solution.py:13
  492.7 26.2 %collective-permute-start.25 = (f32[256,1024]{1,0:T(8,128)S(1)}, f32[256,1024]{1,0:T(8,128)S(1)}, u32[]{:S(2)}, u32[]{:S(2)}) collective-permute-start(f32[256,1024]{1,0:T(8,128)S(1)} %get-tuple-element.15), channel_id=1, source_target_pairs={{0,4},{1,5},{2,6},{3,7},{4,0},{5,1},{6,2},{7,3},{8,12},{9,13},{10,... | collective-permute-start | bytes 3145736 | tf_op jit(solution)/shard_map/ppermute | solution.py:13
  493.5 43.8 %collective-permute-start.26 = (f32[256,1024]{1,0:T(8,128)S(1)}, f32[256,1024]{1,0:T(8,128)S(1)}, u32[]{:S(2)}, u32[]{:S(2)}) collective-permute-start(f32[256,1024]{1,0:T(8,128)S(1)} %get-tuple-element.14), channel_id=1, source_target_pairs={{0,4},{1,5},{2,6},{3,7},{4,0},{5,1},{6,2},{7,3},{8,12},{9,13},{10,... | collective-permute-start | bytes 3145736 | tf_op jit(solution)/shard_map/ppermute | solution.py:13
  538.0 67.4 %collective-permute-start.27 = (f32[256,1024]{1,0:T(8,128)S(1)}, f32[256,1024]{1,0:T(8,128)S(1)}, u32[]{:S(2)}, u32[]{:S(2)}) collective-permute-start(f32[256,1024]{1,0:T(8,128)S(1)} %get-tuple-element.13), channel_id=1, source_target_pairs={{0,8},{1,9},{2,10},{3,11},{4,12},{5,13},{6,14},{7,15},{8,0},{9,1},... | collective-permute-start | bytes 3145736 | tf_op jit(solution)/shard_map/ppermute | solution.py:13
  541.1 84.3 %collective-permute-start.28 = (f32[256,1024]{1,0:T(8,128)S(1)}, f32[256,1024]{1,0:T(8,128)S(1)}, u32[]{:S(2)}, u32[]{:S(2)}) collective-permute-start(f32[256,1024]{1,0:T(8,128)S(1)} %get-tuple-element.12), channel_id=1, source_target_pairs={{0,8},{1,9},{2,10},{3,11},{4,12},{5,13},{6,14},{7,15},{8,0},{9,1},... | collective-permute-start | bytes 3145736 | tf_op jit(solution)/shard_map/ppermute | solution.py:13
  626.0 65.0 %collective-permute-start.29 = (f32[256,1024]{1,0:T(8,128)S(1)}, f32[256,1024]{1,0:T(8,128)S(1)}, u32[]{:S(2)}, u32[]{:S(2)}) collective-permute-start(f32[256,1024]{1,0:T(8,128)S(1)} %get-tuple-element.11), channel_id=1, source_target_pairs={{0,16},{1,17},{2,18},{3,19},{4,20},{5,21},{6,22},{7,23},{8,24},{9,... | collective-permute-start | bytes 3145736 | tf_op jit(solution)/shard_map/ppermute | solution.py:13
  629.7 91.2 %collective-permute-start.30 = (f32[256,1024]{1,0:T(8,128)S(1)}, f32[256,1024]{1,0:T(8,128)S(1)}, u32[]{:S(2)}, u32[]{:S(2)}) collective-permute-start(f32[256,1024]{1,0:T(8,128)S(1)} %get-tuple-element.10), channel_id=1, source_target_pairs={{0,16},{1,17},{2,18},{3,19},{4,20},{5,21},{6,22},{7,23},{8,24},{9,... | collective-permute-start | bytes 3145736 | tf_op jit(solution)/shard_map/ppermute | solution.py:13
  721.3 7.0 collective-permute-start.31
  (7 other events, 309.3 us)
where the time goes:
time: 739 us; the launch traced here: 729 us
  waiting for transfers between devices  610 us (83%)
  starting transfers between devices  61.1 us (8%)
  other arithmetic  23.9 us (3%)
  matrix products  22.7 us (3%)
  local copies, waits for them, and re-layouts  10.6 us (1%)
    ppermute x30, waiting for transfers between devices, partner_2(): lax.ppermute(shard, axis, [(i, i ^ 1 << bit) for i in range(lax.axis_size...  602 us
    ppermute x30, starting transfers between devices, partner_2(): lax.ppermute(shard, axis, [(i, i ^ 1 << bit) for i in range(lax.axis_size...  57.6 us
  transfers between devices with their start and end apart: 32, of which 27 were waited for; matrix products, arithmetic and copies ran while one was open for 3% of the time, Pallas kernels for 0%

commit v1 on v0

v1 whole, which is shorter than its diff:
```python
import functools

import jax
import jax.numpy as jnp
from jax import lax
from jax.experimental import pallas as pl
from jax.experimental.pallas import tpu as pltpu
from jax.sharding import PartitionSpec as P

MESH = pl.DeviceIdType.MESH
HIGHEST = lax.Precision.HIGHEST
F32 = jnp.float32
BF16 = jnp.bfloat16
NX = 4
LANES = 128
STEP = 8


def iota(shape, axis):
    return lax.broadcasted_iota(jnp.int32, shape, axis)


def split(value):
    high = value.astype(BF16)
    return high, (value - high.astype(F32)).astype(BF16)


def dot3(left, right):
    dot = functools.partial(jnp.dot, preferred_element_type=F32)
    return dot(left[0], right[0]) + (dot(left[1], right[0]) + dot(left[0], right[1]))


def mode_scale(residues, decay):
    twice = 2.0 * decay
    series = jnp.full_like(twice, 1.0)
    for order in range(10, 1, -1):
        series = 1.0 - series * twice * (1.0 / order)
    gain = jnp.where(twice < 0.5, twice * series, 1.0 - jnp.exp(-twice))
    return residues * jnp.sqrt(gain)


def over_channels(table, channels):
    groups = table.shape[1]
    pick = (iota((groups, channels), 0) == iota((groups, channels), 1) // (channels // groups)).astype(F32)
    return lax.dot_general(table, pick, (((1,), (0,)), ((), ())), precision=HIGHEST, preferred_element_type=F32)


def flat_row(table):
    modes, groups = table.shape
    size = groups * modes
    pick = (iota((modes, size), 0) == iota((modes, size), 1) % modes).astype(F32)
    spread = lax.dot_general(table, pick, (((0,), (0,)), ((), ())), precision=HIGHEST, preferred_element_type=F32)
    keep = iota((groups, size), 0) == iota((groups, size), 1) // modes
    return jnp.sum(jnp.where(keep, spread, 0.0), axis=0, keepdims=True)


def kernel(
    n_section, n_ctx, rows, channels, groups, modes,
    feat_ref, conv_ref, res_ref, dec_ref, skip_ref, out_ref,
    kv, qlast, own_lam, own_w, gate_hi, gate_lo, outbox, esend, p1, ebox, rsend, p2, acc, pre, hsend, p3,
    fbox, halo, conv_in, res_in, dec_in, skip_in, gated, query, mixed, out_hi, out_lo,
    local_sem, par_send, par_recv, feat_send, feat_recv, halo_send, halo_recv,
    p1_send, p1_recv, edge_send, edge_recv, p2_send, p2_recv, p3_send, p3_recv,
):
    nz = n_ctx // NX
    tiles = channels // LANES
    per = channels // groups
    block = (LANES // per) * modes
    sec = lax.axis_index("section")
    ctx = lax.axis_index("ctx")
    z = ctx // NX
    x = ctx % NX
    sec_next = (sec + 1) % n_section
    sec_prev = (sec + n_section - 1) % n_section

    kv_copy = pltpu.make_async_copy(feat_ref.at[0, :, pl.ds(channels, 2 * channels)], kv, local_sem.at[0])
    kv_copy.start()
    q_copy = pltpu.make_async_copy(feat_ref.at[0, pl.ds(rows - 16, 16), pl.ds(0, channels)], qlast, local_sem.at[1])
    q_copy.start()

    barrier = pltpu.get_barrier_semaphore()

    def greet(section, position):
        pl.semaphore_signal(barrier, inc=1, device_id=(section, position), device_id_type=MESH)

    z_next = (z + 1) % nz
    z_prev = (z + nz - 1) % nz
    for o in range(1, nz):
        greet(sec, ((z + o) % nz) * NX + x)
    for o in range(1, NX):
        greet(sec, z * NX + (x + o) % NX)
        greet(sec, z_next * NX + (x + o) % NX)
        greet(sec, z_prev * NX + (x + o) % NX)
    for o in range(NX):
        greet(sec_next, z * NX + o)
        greet(sec_prev, z * NX + o)

    @pl.when(x == NX - 1)
    def _():
        greet(sec_next, z_next * NX)

    @pl.when(x == 0)
    def _():
        greet(sec_prev, z_prev * NX + NX - 1)

    n_greet = (nz - 1) + 3 * (NX - 1) + 2 * NX

    decay = dec_ref[0]
    scale = mode_scale(res_ref[0], decay)
    lam_wide = over_channels(decay, channels)
    w_wide = over_channels(scale, channels)
    lam_row = flat_row(decay)
    w_row = flat_row(scale)
    for j in range(tiles):
        own_lam[j] = lam_wide[:, j * LANES:(j + 1) * LANES]
        own_w[j] = w_wide[:, j * LANES:(j + 1) * LANES]

    kv_copy.wait()
    q_copy.wait()
    row = iota((rows, LANES), 0)
    to_end = (rows - 1 - row).astype(F32)
    keep = iota((block, LANES), 0) // modes == iota((block, LANES), 1) // per

    for j in range(tiles):
        parts = []
        edges = []
        for part in range(2):
            cols = pl.ds(part * channels + j * LANES, LANES)
            value = kv[:, cols].astype(F32)
            taps = [conv_ref[i, :, pl.ds((part + 1) * channels + j * LANES, LANES)] for i in range(3)]
            parts.append(taps[0] * value + taps[1] * pltpu.roll(value, 1, 0) + taps[2] * pltpu.roll(value, 2, 0))
            edges.append(value)
            esend[:, pl.ds((part + 1) * channels + j * LANES, LANES)] = value[rows - 2:]
        esend[:, pl.ds(j * LANES, LANES)] = qlast[:, pl.ds(j * LANES, LANES)].astype(F32)[14:]
        gate = split(jnp.where(row >= 2, parts[0] * parts[1], 0.0))
        rising = w_row[:, j * block:(j + 1) * block] * jnp.exp(-lam_row[:, j * block:(j + 1) * block] * to_end)
        state = dot3(split(rising.T), gate)
        state = jnp.where(keep, state, 0.0).reshape(block // modes, modes, LANES).sum(axis=0)
        outbox[j, pl.ds(0, modes)] = state
        outbox[j, pl.ds(modes, 8)] = jnp.concatenate(
            [edges[0][rows - 2:], edges[1][rows - 2:], edges[0][:2], edges[1][:2]], axis=0
        )

    pl.semaphore_wait(barrier, n_greet + (x == NX - 1).astype(jnp.int32) + (x == 0).astype(jnp.int32))

    def send(source, target, send_sem, recv_sem, section, position):
        return pltpu.make_async_remote_copy(
            src_ref=source, dst_ref=target, send_sem=send_sem, recv_sem=recv_sem,
            device_id=(section, position), device_id_type=MESH,
        )

    p1_copies = []
    for o in range(1, NX):
        q = (x + o) % NX
        p1_copies.append(send(outbox.at[q], p1.at[o], p1_send.at[o], p1_recv.at[o], sec, z * NX + q))
        p1_copies[-1].start()

    def edge_copy(q):
        return send(
            outbox.at[q, pl.ds(modes, 8)], ebox, edge_send.at[q], edge_recv.at[0], sec,
            (z + 1) % nz * NX + q,
        )

    @pl.when(jnp.logical_and(x == NX - 1, z < nz - 1))
    def _():
        for q in range(NX):
            edge_copy(q).start()

    ship = []
    for n, (source, target) in enumerate(((conv_ref, conv_in), (res_ref, res_in), (dec_ref, dec_in), (skip_ref, skip_in))):
        ship.append(send(source, target, par_send.at[n], par_recv.at[n], sec_next, ctx))
    feat_copies = []
    for j in range(tiles):
        for part in range(3):
            feat_copies.append(
                send(
                    feat_ref.at[0, :, pl.ds(part * channels + j * LANES, LANES)], fbox.at[j, part],
                    feat_send.at[j, part], feat_recv.at[j, part], sec_next, ctx,
                )
            )
    halo_copy = send(esend, halo, halo_send.at[0], halo_recv.at[0], sec_next, (ctx + 1) % n_ctx)
    for copy in ship + [halo_copy] + feat_copies:
        copy.start()

    p1[0] = outbox[x]

    @pl.when(z == 0)
    def _():
        ebox[...] = jnp.zeros_like(ebox)

    acc[...] = jnp.zeros_like(acc)
    lam = own_lam[x]
    w_own = own_w[x]
    for copy in p1_copies:
        copy.wait_recv()

    @pl.when(z > 0)
    def _():
        edge_copy(0).wait_recv()

    span = float(rows)
    fade_row = jnp.exp(-span * lam)
    first = w_own * jnp.exp(-(span - 1.0) * lam)
    second = w_own * jnp.exp(-(span - 2.0) * lam)
    taps = [
        [conv_ref[i, :, pl.ds(pl.multiple_of((part + 1) * channels + x * LANES, LANES), LANES)] for i in range(3)]
        for part in range(2)
    ]
    before = ebox[...]
    total = jnp.zeros((modes, LANES), F32)
    for member in range(NX):
        slot = (x + NX - member) % NX
        edge = p1[slot, pl.ds(modes, 8)]
        products = []
        for part in range(2):
            old2 = before[2 * part:2 * part + 1]
            old1 = before[2 * part + 1:2 * part + 2]
            new0 = edge[4 + 2 * part:5 + 2 * part]
            new1 = edge[5 + 2 * part:6 + 2 * part]
            t0, t1, t2 = taps[part]
            products.append((t0 * new0 + t1 * old1 + t2 * old2, t0 * new1 + t1 * new0 + t2 * old1))
        state = p1[slot, pl.ds(0, modes)]
        state = state + first * (products[0][0] * products[1][0]) + second * (products[0][1] * products[1][1])
        pre[member] = total
        total = fade_row * total + state
        before = edge
    rsend[...] = total

    def p2_copy(o):
        return send(rsend, p2.at[o], p2_send.at[o], p2_recv.at[o], sec, (z + o) % nz * NX + x)

    order = sorted(range(1, nz), key=lambda o: (-min(o, nz - o), o))
    for o in order:
        @pl.when(z + o < nz)
        def _(o=o):
            p2_copy(o).start()

    for copy in ship:
        copy.wait_recv()
    halo_copy.wait_recv()

    @pl.when(ctx == 0)
    def _():
        halo[...] = jnp.zeros_like(halo)

    decay_in = dec_in[0]
    scale_in = mode_scale(res_in[0], decay_in)
    lam_in = over_channels(decay_in, channels)
    w_in = over_channels(scale_in, channels)
    row_in = flat_row(decay_in)
    for j in range(tiles):
        falling = jnp.exp(-row_in[:, j * block:(j + 1) * block] * (row + 1).astype(F32))
        high, low = split(falling)
        out_hi[:, pl.ds(j * block, block)] = high
        out_lo[:, pl.ds(j * block, block)] = low

    def local_tile(j):
        cols = pl.ds(j * LANES, LANES)
        for part in range(3):
            feat_copies[3 * j + part].wait_recv()
        shaped = []
        for part in range(3):
            value = fbox[j, part].astype(F32)
            wide = pl.ds(part * channels + j * LANES, LANES)
            edge = halo[:, wide]
            one = jnp.where(row == 0, edge[1:2], pltpu.roll(value, 1, 0))
            two = jnp.where(row == 0, edge[0:1], jnp.where(row == 1, edge[1:2], pltpu.roll(value, 2, 0)))
            t0, t1, t2 = [conv_in[i, :, wide] for i in range(3)]
            shaped.append(t0 * value + t1 * one + t2 * two)
        query[:, cols] = shaped[0]
        gated[:, cols] = shaped[1] * shaped[2]
        lam_j = lam_in[:, j * LANES:(j + 1) * LANES]
        w_j = w_in[:, j * LANES:(j + 1) * LANES]
        gain = skip_in[:, cols]
        step_row = iota((STEP, LANES), 0)
        near = []
        enter = []
        for i in range(STEP):
            faded = w_j * jnp.exp(-float(i) * lam_j)
            tap = jnp.sum(faded, axis=0, keepdims=True)
            near.append(jnp.where(step_row >= i, tap, 0.0))
            enter.append(faded)
        near[0] = near[0] + gain
        ahead = (step_row + 1).astype(F32)
        leave = [jnp.exp(-lam_j[m:m + 1] * ahead) for m in range(modes)]
        fade = jnp.exp(-float(STEP) * lam_j)

        def body(k, state):
            at = pl.ds(pl.multiple_of(k * STEP, STEP), STEP)
            now = gated[at, cols]
            value = near[0] * now
            for i in range(1, STEP):
                value = value + near[i] * pltpu.roll(now, i, 0)
            for m in range(modes):
                value = value + leave[m] * state[m:m + 1]
            mixed[at, cols] = value
            state = fade * state
            for i in range(STEP):
                state = state + enter[STEP - 1 - i] * now[i:i + 1]
            return state

        lax.fori_loop(0, rows // STEP, body, jnp.zeros((modes, LANES), F32))

    for j in range(tiles // 2):
        local_tile(j)

    fade_z = jnp.exp(-(span * NX) * lam)
    for o in range(nz - 1, 0, -1):
        @pl.when(z >= o)
        def _(o=o):
            p2_copy(o).wait_recv()
            acc[...] = fade_z * acc[...] + p2[o]

    carry = acc[...]
    p3_copies = []
    for member in range(NX):
        hsend[member] = carry + pre[member]
        carry = fade_row * carry
        p3_copies.append(
            send(hsend.at[member], p3.at[x], p3_send.at[member], p3_recv.at[x], sec_next, z * NX + member)
        )
        p3_copies[-1].start()

    for j in range(tiles // 2, tiles):
        local_tile(j)

    for j in range(tiles):
        cols = pl.ds(j * LANES, LANES)
        send(hsend.at[0], p3.at[j], p3_send.at[0], p3_recv.at[j], sec_next, ctx).wait_recv()
        state = p3[j]
        spread = jnp.where(keep, jnp.concatenate([state] * (block // modes), axis=0), 0.0)
        wide = pl.ds(j * block, block)
        carried = dot3((out_hi[:, wide], out_lo[:, wide]), split(spread))
        out_ref[0, :, cols] = (query[:, cols] * (mixed[:, cols] + carried)).astype(BF16)

    for copy in ship + [halo_copy] + feat_copies + p1_copies + p3_copies:
        copy.wait_send()

    @pl.when(jnp.logical_and(x == NX - 1, z < nz - 1))
    def _():
        for q in range(NX):
            edge_copy(q).wait_send()

    for o in range(1, nz):
        @pl.when(z + o < nz)
        def _(o=o):
            p2_copy(o).wait_send()


def on_device(n_section, n_ctx, features, conv_weight, residues, decay_rates, skip_gain):
    _, rows, width = features.shape
    channels = skip_gain.shape[1]
    _, groups, modes = residues.shape
    tiles = channels // LANES
    nz = n_ctx // NX
    vmem = pltpu.VMEM
    dma = pltpu.SemaphoreType.DMA
    whole = pl.BlockSpec(memory_space=pltpu.VMEM)
    conv_weight = jnp.swapaxes(conv_weight, 0, 1)
    residues = jnp.swapaxes(residues, 1, 2)
    decay_rates = jnp.swapaxes(decay_rates, 1, 2)
    return pl.pallas_call(
        functools.partial(kernel, n_section, n_ctx, rows, channels, groups, modes),
        out_shape=jax.ShapeDtypeStruct((1, rows, channels), BF16),
        in_specs=[pl.BlockSpec(memory_space=pl.ANY)] + [whole] * 4,
        out_specs=whole,
        scratch_shapes=[
            vmem((rows, 2 * channels), BF16),
            vmem((16, channels), BF16),
            vmem((tiles, modes, LANES), F32),
            vmem((tiles, modes, LANES), F32),
            vmem((rows, LANES), BF16),
            vmem((rows, LANES), BF16),
            vmem((tiles, modes + 8, LANES), F32),
            vmem((2, width), F32),
            vmem((NX, modes + 8, LANES), F32),
            vmem((8, LANES), F32),
            vmem((modes, LANES), F32),
            vmem((nz, modes, LANES), F32),
            vmem((modes, LANES), F32),
            vmem((NX, modes, LANES), F32),
            vmem((NX, modes, LANES), F32),
            vmem((tiles, modes, LANES), F32),
            vmem((tiles, 3, rows, LANES), BF16),
            vmem((2, width), F32),
            vmem(conv_weight.shape, F32),
            vmem(residues.shape, F32),
            vmem(decay_rates.shape, F32),
            vmem(skip_gain.shape, F32),
            vmem((rows, channels), F32),
            vmem((rows, channels), F32),
            vmem((rows, channels), F32),
            vmem((rows, groups * modes), BF16),
            vmem((rows, groups * modes), BF16),
            dma((2,)),
            dma((4,)), dma((4,)),
            dma((tiles, 3)), dma((tiles, 3)),
            dma((1,)), dma((1,)),
            dma((NX,)), dma((NX,)),
            dma((NX,)), dma((1,)),
            dma((nz,)), dma((nz,)),
            dma((NX,)), dma((NX,)),
        ],
        compiler_params=pltpu.CompilerParams(collective_id=0, has_side_effects=True),
        name="mixer",
    )(features, conv_weight, residues, decay_rates, skip_gain)


def solution(mesh):
    placed = (
        P("section", "ctx", None),
        P("section", None, None),
        P("section", None, None),
        P("section", None, None),
        P("section", None),
    )
    body = functools.partial(on_device, mesh.shape["section"], mesh.shape["ctx"])
    return jax.shard_map(body, mesh=mesh, in_specs=placed, out_specs=P("section", "ctx", None), check_vma=False)
```

time: 739 us -> 26.4 us (0.04); the launches traced: 729 us -> 25.9 us
  waiting for transfers between devices: 610 us -> 0 us
  starting transfers between devices: 61.1 us -> 0 us
  Pallas kernels: 0 us -> 24.2 us
  other arithmetic: 23.9 us -> 0 us
  matrix products: 22.7 us -> 0 us
  local copies, waits for them, and re-layouts: 10.6 us -> 1.67 us
    ppermute x32 -> x0, waiting for transfers between devices: 610 us -> none  [the longest x30 602 us: partner_2(): lax.ppermute(shard, axis, [(i, i ^ 1 << bit) for i in range(lax.axis_size...]
    ppermute x32 -> x0, starting transfers between devices: 61.1 us -> none  [the longest x30 57.6 us: partner_2(): lax.ppermute(shard, axis, [(i, i ^ 1 << bit) for i in range(lax.axis_size...]
    pallas_call x0 -> x1, Pallas kernels: none -> 24.2 us  [on_device(): pl.pallas_call(functools.partial(kernel, n_section, n_ctx, rows, channels...]
    dot_general x12 -> x0, matrix products: 22.7 us -> none  [the longest x3 5.83 us: complex_apply(): matmul(sines, real_part)]
    select_n x14 -> x0, other arithmetic: 18.6 us -> none  [the longest x5 14.2 us: forward_pairwise(): jnp.where(is_upper, pieces[offset + 1] + partner[offset + 1], turned_im)]
  transfers between devices with their start and end apart: 32 -> 0, of which waited for: 27 -> 0; matrix products, arithmetic and copies ran while one was open for 3% -> 0% of each run, Pallas kernels for 0% -> 0%
where the time goes in v1:
time: 26.4 us; the launch traced here: 25.9 us
  Pallas kernels  24.2 us (92%)
  local copies, waits for them, and re-layouts  1.67 us (6%)
    pallas_call x1, Pallas kernels, on_device(): pl.pallas_call(functools.partial(kernel, n_section, n_ctx, rows, channels...  24.2 us
    unnamed x1, local copies, waits for them, and re-layouts  1.67 us

profile of v1, /device:TPU:2, one launch (start us, length us, event | category | flops | bytes accessed | tf_op | source)
XLA Modules:
  0.0 25.9 jit_solution(13221519300603210638)
XLA Ops:
  0.0 24.2 %mixer.1 = bf16[1,256,512]{2,1,0:T(8,128)(2,1)} custom-call(bf16[1,256,1536]{2,1,0:T(8,128)(2,1)} %feat_ref.1, f32[3,1,1536]{2,1,0:T(1,128)} %bitcast.3, f32[1,16,32]{2,1,0:T(8,128)} %bitcast.4, f32[1,16,32]{2,1,0:T(8,128)} %bitcast.5, f32[1,512]{1,0:T(1,128)} %skip_ref.1), custom_call_target="tpu_custom_call" | custom-call | tf_op jit(solution)/shard_map/mixer/pallas_call | solution.py:362
  24.2 1.7 %copy.7 = bf16[1,256,512]{2,1,0:T(8,128)(2,1)} copy(bf16[1,256,512]{2,1,0:T(8,128)(2,1)} %mixer.1) | data formatting | bytes 524288

commit v2 on v1

--- a/solution.py
+++ b/solution.py
@@ -13,7 +13,7 @@
 BF16 = jnp.bfloat16
 NX = 4
 LANES = 128
-STEP = 8
+CHUNKS = 8
 
 
 def iota(shape, axis):
@@ -64,6 +64,7 @@
 ):
     nz = n_ctx // NX
     tiles = channels // LANES
+    length = rows // CHUNKS
     per = channels // groups
     block = (LANES // per) * modes
     sec = lax.axis_index("section")
@@ -268,38 +269,50 @@
             t0, t1, t2 = [conv_in[i, :, wide] for i in range(3)]
             shaped.append(t0 * value + t1 * one + t2 * two)
         query[:, cols] = shaped[0]
-        gated[:, cols] = shaped[1] * shaped[2]
+        gated[...] = shaped[1] * shaped[2]
         lam_j = lam_in[:, j * LANES:(j + 1) * LANES]
         w_j = w_in[:, j * LANES:(j + 1) * LANES]
-        gain = skip_in[:, cols]
-        step_row = iota((STEP, LANES), 0)
-        near = []
-        enter = []
-        for i in range(STEP):
-            faded = w_j * jnp.exp(-float(i) * lam_j)
-            tap = jnp.sum(faded, axis=0, keepdims=True)
-            near.append(jnp.where(step_row >= i, tap, 0.0))
-            enter.append(faded)
-        near[0] = near[0] + gain
-        ahead = (step_row + 1).astype(F32)
-        leave = [jnp.exp(-lam_j[m:m + 1] * ahead) for m in range(modes)]
-        fade = jnp.exp(-float(STEP) * lam_j)
-
-        def body(k, state):
-            at = pl.ds(pl.multiple_of(k * STEP, STEP), STEP)
-            now = gated[at, cols]
-            value = near[0] * now
-            for i in range(1, STEP):
-                value = value + near[i] * pltpu.roll(now, i, 0)
-            for m in range(modes):
-                value = value + leave[m] * state[m:m + 1]
-            mixed[at, cols] = value
-            state = fade * state
-            for i in range(STEP):
-                state = state + enter[STEP - 1 - i] * now[i:i + 1]
-            return state
-
-        lax.fori_loop(0, rows // STEP, body, jnp.zeros((modes, LANES), F32))
+        gain = jnp.broadcast_to(skip_in[:, cols], (CHUNKS, LANES))
+        chunk = iota((CHUNKS, LANES), 0)
+
+        def lines(table):
+            return [jnp.broadcast_to(table[m:m + 1], (CHUNKS, LANES)) for m in range(modes)]
+
+        def total(values):
+            while len(values) > 1:
+                values = [a + b for a, b in zip(values[::2], values[1::2])]
+            return values[0]
+
+        fade = lines(jnp.exp(-lam_j))
+        weight = lines(w_j)
+
+        def inside(r, states):
+            at = pl.ds(r, CHUNKS, stride=length)
+            now = gated[at, :]
+            states = [fade[m] * states[m] + weight[m] * now for m in range(modes)]
+            mixed[j, at, :] = gain * now + total(states)
+            return tuple(states)
+
+        states = lax.fori_loop(
+            0, length, inside, tuple(jnp.zeros((CHUNKS, LANES), F32) for _ in range(modes)), unroll=4
+        )
+
+        shift = 1
+        while shift < CHUNKS:
+            over = lines(jnp.exp(-float(length * shift) * lam_j))
+            states = [
+                states[m] + jnp.where(chunk >= shift, over[m] * pltpu.roll(states[m], shift, 0), 0.0)
+                for m in range(modes)
+            ]
+            shift *= 2
+        states = tuple(fade[m] * jnp.where(chunk >= 1, pltpu.roll(states[m], 1, 0), 0.0) for m in range(modes))
+
+        def across(r, states):
+            at = pl.ds(r, CHUNKS, stride=length)
+            mixed[j, at, :] = mixed[j, at, :] + total(list(states))
+            return tuple(fade[m] * states[m] for m in range(modes))
+
+        lax.fori_loop(0, length, across, states, unroll=4)
 
     for j in range(tiles // 2):
         local_tile(j)
@@ -325,13 +338,14 @@
         local_tile(j)
 
     for j in range(tiles):
+        send(hsend.at[0], p3.at[j], p3_send.at[0], p3_recv.at[j], sec_next, ctx).wait_recv()
+    for j in range(tiles):
         cols = pl.ds(j * LANES, LANES)
-        send(hsend.at[0], p3.at[j], p3_send.at[0], p3_recv.at[j], sec_next, ctx).wait_recv()
         state = p3[j]
         spread = jnp.where(keep, jnp.concatenate([state] * (block // modes), axis=0), 0.0)
         wide = pl.ds(j * block, block)
         carried = dot3((out_hi[:, wide], out_lo[:, wide]), split(spread))
-        out_ref[0, :, cols] = (query[:, cols] * (mixed[:, cols] + carried)).astype(BF16)
+        out_ref[0, :, cols] = (query[:, cols] * (mixed[j] + carried)).astype(BF16)
 
     for copy in ship + [halo_copy] + feat_copies + p1_copies + p3_copies:
         copy.wait_send()
@@ -361,7 +375,7 @@
     decay_rates = jnp.swapaxes(decay_rates, 1, 2)
     return pl.pallas_call(
         functools.partial(kernel, n_section, n_ctx, rows, channels, groups, modes),
-        out_shape=jax.ShapeDtypeStruct((1, rows, channels), BF16),
+        out_shape=pltpu.VMEM((1, rows, channels), BF16),
         in_specs=[pl.BlockSpec(memory_space=pl.ANY)] + [whole] * 4,
         out_specs=whole,
         scratch_shapes=[
@@ -387,9 +401,9 @@
             vmem(residues.shape, F32),
             vmem(decay_rates.shape, F32),
             vmem(skip_gain.shape, F32),
+            vmem((rows, LANES), F32),
             vmem((rows, channels), F32),
-            vmem((rows, channels), F32),
-            vmem((rows, channels), F32),
+            vmem((tiles, rows, LANES), F32),
             vmem((rows, groups * modes), BF16),
             vmem((rows, groups * modes), BF16),
             dma((2,)),

time: 26.4 us -> 24.4 us (0.924)
  the two profiles are of different devices: /device:TPU:2 before, /device:TPU:1 now
where the time goes in v2:
time: 24.4 us; the launch traced here: 24.3 us
  Pallas kernels  23.6 us (97%)
  local copies, waits for them, and re-layouts  0.71 us (3%)
    pallas_call x1, Pallas kernels, on_device(): pl.pallas_call(functools.partial(kernel, n_section, n_ctx, rows, channels...  23.6 us
    unnamed x1, local copies, waits for them, and re-layouts  0.71 us

profile of v2, /device:TPU:1, one launch (start us, length us, event | category | flops | bytes accessed | tf_op | source)
XLA Modules:
  0.0 24.3 jit_solution(7051360175747819362)
XLA Ops:
  0.0 23.6 %mixer.1 = bf16[1,256,512]{2,1,0:T(8,128)(2,1)S(1)} custom-call(bf16[1,256,1536]{2,1,0:T(8,128)(2,1)} %feat_ref.1, f32[3,1,1536]{2,1,0:T(1,128)} %bitcast.3, f32[1,16,32]{2,1,0:T(8,128)} %bitcast.4, f32[1,16,32]{2,1,0:T(8,128)} %bitcast.5, f32[1,512]{1,0:T(1,128)} %skip_ref.1), custom_call_target="tpu_custom_call" | custom-call | tf_op jit(solution)/shard_map/mixer/pallas_call | solution.py:376
  23.6 0.7 %copy.7 = bf16[1,256,512]{2,1,0:T(8,128)(2,1)} copy(bf16[1,256,512]{2,1,0:T(8,128)(2,1)S(1)} %mixer.1) | data formatting | bytes 524288

commit v3 on v2

--- a/solution.py
+++ b/solution.py
@@ -60,7 +60,7 @@
     kv, qlast, own_lam, own_w, gate_hi, gate_lo, outbox, esend, p1, ebox, rsend, p2, acc, pre, hsend, p3,
     fbox, halo, conv_in, res_in, dec_in, skip_in, gated, query, mixed, out_hi, out_lo,
     local_sem, par_send, par_recv, feat_send, feat_recv, halo_send, halo_recv,
-    p1_send, p1_recv, edge_send, edge_recv, p2_send, p2_recv, p3_send, p3_recv,
+    p1_send, p1_recv, edge_send, edge_recv, p2_send, p2_recv, p3_send, p3_recv, here,
 ):
     nz = n_ctx // NX
     tiles = channels // LANES
@@ -86,13 +86,11 @@
 
     z_next = (z + 1) % nz
     z_prev = (z + nz - 1) % nz
-    for o in range(1, nz):
-        greet(sec, ((z + o) % nz) * NX + x)
     for o in range(1, NX):
         greet(sec, z * NX + (x + o) % NX)
-        greet(sec, z_next * NX + (x + o) % NX)
-        greet(sec, z_prev * NX + (x + o) % NX)
     for o in range(NX):
+        greet(sec, z_next * NX + o)
+        greet(sec, z_prev * NX + o)
         greet(sec_next, z * NX + o)
         greet(sec_prev, z * NX + o)
 
@@ -104,7 +102,7 @@
     def _():
         greet(sec_prev, z_prev * NX + NX - 1)
 
-    n_greet = (nz - 1) + 3 * (NX - 1) + 2 * NX
+    n_greet = (NX - 1) + 4 * NX
 
     decay = dec_ref[0]
     scale = mode_scale(res_ref[0], decay)
@@ -122,25 +120,8 @@
     to_end = (rows - 1 - row).astype(F32)
     keep = iota((block, LANES), 0) // modes == iota((block, LANES), 1) // per
 
-    for j in range(tiles):
-        parts = []
-        edges = []
-        for part in range(2):
-            cols = pl.ds(part * channels + j * LANES, LANES)
-            value = kv[:, cols].astype(F32)
-            taps = [conv_ref[i, :, pl.ds((part + 1) * channels + j * LANES, LANES)] for i in range(3)]
-            parts.append(taps[0] * value + taps[1] * pltpu.roll(value, 1, 0) + taps[2] * pltpu.roll(value, 2, 0))
-            edges.append(value)
-            esend[:, pl.ds((part + 1) * channels + j * LANES, LANES)] = value[rows - 2:]
-        esend[:, pl.ds(j * LANES, LANES)] = qlast[:, pl.ds(j * LANES, LANES)].astype(F32)[14:]
-        gate = split(jnp.where(row >= 2, parts[0] * parts[1], 0.0))
-        rising = w_row[:, j * block:(j + 1) * block] * jnp.exp(-lam_row[:, j * block:(j + 1) * block] * to_end)
-        state = dot3(split(rising.T), gate)
-        state = jnp.where(keep, state, 0.0).reshape(block // modes, modes, LANES).sum(axis=0)
-        outbox[j, pl.ds(0, modes)] = state
-        outbox[j, pl.ds(modes, 8)] = jnp.concatenate(
-            [edges[0][rows - 2:], edges[1][rows - 2:], edges[0][:2], edges[1][:2]], axis=0
-        )
+    esend[:, pl.ds(0, channels)] = qlast[...].astype(F32)[14:]
+    esend[:, pl.ds(channels, 2 * channels)] = kv[pl.ds(rows - 16, 16), :].astype(F32)[14:]
 
     pl.semaphore_wait(barrier, n_greet + (x == NX - 1).astype(jnp.int32) + (x == 0).astype(jnp.int32))
 
@@ -150,22 +131,12 @@
             device_id=(section, position), device_id_type=MESH,
         )
 
-    p1_copies = []
-    for o in range(1, NX):
-        q = (x + o) % NX
-        p1_copies.append(send(outbox.at[q], p1.at[o], p1_send.at[o], p1_recv.at[o], sec, z * NX + q))
-        p1_copies[-1].start()
-
-    def edge_copy(q):
-        return send(
-            outbox.at[q, pl.ds(modes, 8)], ebox, edge_send.at[q], edge_recv.at[0], sec,
-            (z + 1) % nz * NX + q,
-        )
-
-    @pl.when(jnp.logical_and(x == NX - 1, z < nz - 1))
-    def _():
-        for q in range(NX):
-            edge_copy(q).start()
+    def pass_on(n):
+        for row_of in (z_next, z_prev):
+            pl.semaphore_signal(here.at[n], inc=1, device_id=(sec, row_of * NX + x), device_id_type=MESH)
+
+    rounds = nz // 2 - 1
+    pass_on(0)
 
     ship = []
     for n, (source, target) in enumerate(((conv_ref, conv_in), (res_ref, res_in), (dec_ref, dec_in), (skip_ref, skip_in))):
@@ -183,6 +154,45 @@
     for copy in ship + [halo_copy] + feat_copies:
         copy.start()
 
+    for j in range(tiles):
+        parts = []
+        edges = []
+        for part in range(2):
+            cols = pl.ds(part * channels + j * LANES, LANES)
+            value = kv[:, cols].astype(F32)
+            taps = [conv_ref[i, :, pl.ds((part + 1) * channels + j * LANES, LANES)] for i in range(3)]
+            parts.append(taps[0] * value + taps[1] * pltpu.roll(value, 1, 0) + taps[2] * pltpu.roll(value, 2, 0))
+            edges.append(value)
+        gate = split(jnp.where(row >= 2, parts[0] * parts[1], 0.0))
+        rising = w_row[:, j * block:(j + 1) * block] * jnp.exp(-lam_row[:, j * block:(j + 1) * block] * to_end)
+        state = dot3(split(rising.T), gate)
+        state = jnp.where(keep, state, 0.0).reshape(block // modes, modes, LANES).sum(axis=0)
+        outbox[j, pl.ds(0, modes)] = state
+        outbox[j, pl.ds(modes, 8)] = jnp.concatenate(
+            [edges[0][rows - 2:], edges[1][rows - 2:], edges[0][:2], edges[1][:2]], axis=0
+        )
+
+    pl.semaphore_wait(here.at[0], 2)
+    if rounds > 1:
+        pass_on(1)
+
+    p1_copies = []
+    for o in range(1, NX):
+        q = (x + o) % NX
+        p1_copies.append(send(outbox.at[q], p1.at[o], p1_send.at[o], p1_recv.at[o], sec, z * NX + q))
+        p1_copies[-1].start()
+
+    def edge_copy(q):
+        return send(
+            outbox.at[q, pl.ds(modes, 8)], ebox, edge_send.at[q], edge_recv.at[0], sec,
+            (z + 1) % nz * NX + q,
+        )
+
+    @pl.when(jnp.logical_and(x == NX - 1, z < nz - 1))
+    def _():
+        for q in range(NX):
+            edge_copy(q).start()
+
     p1[0] = outbox[x]
 
     @pl.when(z == 0)
@@ -192,6 +202,10 @@
     acc[...] = jnp.zeros_like(acc)
     lam = own_lam[x]
     w_own = own_w[x]
+    for n in range(1, rounds):
+        pl.semaphore_wait(here.at[n], 2)
+        if n + 1 < rounds:
+            pass_on(n + 1)
     for copy in p1_copies:
         copy.wait_recv()
 
@@ -414,6 +428,7 @@
             dma((NX,)), dma((1,)),
             dma((nz,)), dma((nz,)),
             dma((NX,)), dma((NX,)),
+            pltpu.SemaphoreType.REGULAR((nz // 2 - 1,)),
         ],
         compiler_params=pltpu.CompilerParams(collective_id=0, has_side_effects=True),
         name="mixer",

time: 24.4 us -> 24 us (0.984)
  Pallas kernels: 23.6 us -> 23.1 us
    pallas_call x1, Pallas kernels: 23.6 us -> 23.1 us  [on_device(): pl.pallas_call(functools.partial(kernel, n_section, n_ctx, rows, channels...]
where the time goes in v3:
time: 24 us; the launch traced here: 23.8 us
  Pallas kernels  23.1 us (96%)
  local copies, waits for them, and re-layouts  0.71 us (3%)
    pallas_call x1, Pallas kernels, on_device(): pl.pallas_call(functools.partial(kernel, n_section, n_ctx, rows, channels...  23.1 us
    unnamed x1, local copies, waits for them, and re-layouts  0.71 us

profile of v3, /device:TPU:1, one launch (start us, length us, event | category | flops | bytes accessed | tf_op | source)
XLA Modules:
  0.0 23.8 jit_solution(16329585166951293925)
XLA Ops:
  0.0 23.1 %mixer.1 = bf16[1,256,512]{2,1,0:T(8,128)(2,1)S(1)} custom-call(bf16[1,256,1536]{2,1,0:T(8,128)(2,1)} %feat_ref.1, f32[3,1,1536]{2,1,0:T(1,128)} %bitcast.3, f32[1,16,32]{2,1,0:T(8,128)} %bitcast.4, f32[1,16,32]{2,1,0:T(8,128)} %bitcast.5, f32[1,512]{1,0:T(1,128)} %skip_ref.1), custom_call_target="tpu_custom_call" | custom-call | tf_op jit(solution)/shard_map/mixer/pallas_call | solution.py:390
  23.1 0.7 %copy.7 = bf16[1,256,512]{2,1,0:T(8,128)(2,1)} copy(bf16[1,256,512]{2,1,0:T(8,128)(2,1)S(1)} %mixer.1) | data formatting | bytes 524288

commit v4 on v2

--- a/solution.py
+++ b/solution.py
@@ -60,7 +60,7 @@
     kv, qlast, own_lam, own_w, gate_hi, gate_lo, outbox, esend, p1, ebox, rsend, p2, acc, pre, hsend, p3,
     fbox, halo, conv_in, res_in, dec_in, skip_in, gated, query, mixed, out_hi, out_lo,
     local_sem, par_send, par_recv, feat_send, feat_recv, halo_send, halo_recv,
-    p1_send, p1_recv, edge_send, edge_recv, p2_send, p2_recv, p3_send, p3_recv,
+    p1_send, p1_recv, edge_send, edge_recv, p2_send, p2_recv, p3_send, p3_recv, here,
 ):
     nz = n_ctx // NX
     tiles = channels // LANES
@@ -86,13 +86,11 @@
 
     z_next = (z + 1) % nz
     z_prev = (z + nz - 1) % nz
-    for o in range(1, nz):
-        greet(sec, ((z + o) % nz) * NX + x)
     for o in range(1, NX):
         greet(sec, z * NX + (x + o) % NX)
-        greet(sec, z_next * NX + (x + o) % NX)
-        greet(sec, z_prev * NX + (x + o) % NX)
     for o in range(NX):
+        greet(sec, z_next * NX + o)
+        greet(sec, z_prev * NX + o)
         greet(sec_next, z * NX + o)
         greet(sec_prev, z * NX + o)
 
@@ -104,7 +102,7 @@
     def _():
         greet(sec_prev, z_prev * NX + NX - 1)
 
-    n_greet = (nz - 1) + 3 * (NX - 1) + 2 * NX
+    n_greet = (NX - 1) + 4 * NX
 
     decay = dec_ref[0]
     scale = mode_scale(res_ref[0], decay)
@@ -121,6 +119,9 @@
     row = iota((rows, LANES), 0)
     to_end = (rows - 1 - row).astype(F32)
     keep = iota((block, LANES), 0) // modes == iota((block, LANES), 1) // per
+
+    esend[:, pl.ds(0, channels)] = qlast[...].astype(F32)[14:]
+    esend[:, pl.ds(channels, 2 * channels)] = kv[pl.ds(rows - 16, 16), :].astype(F32)[14:]
 
     for j in range(tiles):
         parts = []
@@ -131,8 +132,6 @@
             taps = [conv_ref[i, :, pl.ds((part + 1) * channels + j * LANES, LANES)] for i in range(3)]
             parts.append(taps[0] * value + taps[1] * pltpu.roll(value, 1, 0) + taps[2] * pltpu.roll(value, 2, 0))
             edges.append(value)
-            esend[:, pl.ds((part + 1) * channels + j * LANES, LANES)] = value[rows - 2:]
-        esend[:, pl.ds(j * LANES, LANES)] = qlast[:, pl.ds(j * LANES, LANES)].astype(F32)[14:]
         gate = split(jnp.where(row >= 2, parts[0] * parts[1], 0.0))
         rising = w_row[:, j * block:(j + 1) * block] * jnp.exp(-lam_row[:, j * block:(j + 1) * block] * to_end)
         state = dot3(split(rising.T), gate)
@@ -149,6 +148,13 @@
             src_ref=source, dst_ref=target, send_sem=send_sem, recv_sem=recv_sem,
             device_id=(section, position), device_id_type=MESH,
         )
+
+    def pass_on(n):
+        for row_of in (z_next, z_prev):
+            pl.semaphore_signal(here.at[n], inc=1, device_id=(sec, row_of * NX + x), device_id_type=MESH)
+
+    rounds = nz // 2 - 1
+    pass_on(0)
 
     p1_copies = []
     for o in range(1, NX):
@@ -183,6 +189,10 @@
     for copy in ship + [halo_copy] + feat_copies:
         copy.start()
 
+    pl.semaphore_wait(here.at[0], 2)
+    if rounds > 1:
+        pass_on(1)
+
     p1[0] = outbox[x]
 
     @pl.when(z == 0)
@@ -192,6 +202,10 @@
     acc[...] = jnp.zeros_like(acc)
     lam = own_lam[x]
     w_own = own_w[x]
+    for n in range(1, rounds):
+        pl.semaphore_wait(here.at[n], 2)
+        if n + 1 < rounds:
+            pass_on(n + 1)
     for copy in p1_copies:
         copy.wait_recv()
 
@@ -314,8 +328,7 @@
 
         lax.fori_loop(0, length, across, states, unroll=4)
 
-    for j in range(tiles // 2):
-        local_tile(j)
+    local_tile(0)
 
     fade_z = jnp.exp(-(span * NX) * lam)
     for o in range(nz - 1, 0, -1):
@@ -334,7 +347,7 @@
         )
         p3_copies[-1].start()
 
-    for j in range(tiles // 2, tiles):
+    for j in range(1, tiles):
         local_tile(j)
 
     for j in range(tiles):
@@ -414,6 +427,7 @@
             dma((NX,)), dma((1,)),
             dma((nz,)), dma((nz,)),
             dma((NX,)), dma((NX,)),
+            pltpu.SemaphoreType.REGULAR((nz // 2 - 1,)),
         ],
         compiler_params=pltpu.CompilerParams(collective_id=0, has_side_effects=True),
         name="mixer",

time: 24.4 us -> 23.6 us (0.967)
  the two profiles are of different devices: /device:TPU:1 before, /device:TPU:2 now
where the time goes in v4:
time: 23.6 us; the launch traced here: 23.5 us
  Pallas kernels  22.7 us (96%)
  local copies, waits for them, and re-layouts  0.71 us (3%)
    pallas_call x1, Pallas kernels, on_device(): pl.pallas_call(functools.partial(kernel, n_section, n_ctx, rows, channels...  22.7 us
    unnamed x1, local copies, waits for them, and re-layouts  0.71 us

profile of v4, /device:TPU:2, one launch (start us, length us, event | category | flops | bytes accessed | tf_op | source)
XLA Modules:
  0.0 23.5 jit_solution(6005503039112822096)
XLA Ops:
  0.0 22.7 %mixer.1 = bf16[1,256,512]{2,1,0:T(8,128)(2,1)S(1)} custom-call(bf16[1,256,1536]{2,1,0:T(8,128)(2,1)} %feat_ref.1, f32[3,1,1536]{2,1,0:T(1,128)} %bitcast.3, f32[1,16,32]{2,1,0:T(8,128)} %bitcast.4, f32[1,16,32]{2,1,0:T(8,128)} %bitcast.5, f32[1,512]{1,0:T(1,128)} %skip_ref.1), custom_call_target="tpu_custom_call" | custom-call | tf_op jit(solution)/shard_map/mixer/pallas_call | solution.py:389
  22.8 0.7 %copy.7 = bf16[1,256,512]{2,1,0:T(8,128)(2,1)} copy(bf16[1,256,512]{2,1,0:T(8,128)(2,1)S(1)} %mixer.1) | data formatting | bytes 524288

commit v5 on v4

--- a/solution.py
+++ b/solution.py
@@ -177,14 +177,13 @@
     for n, (source, target) in enumerate(((conv_ref, conv_in), (res_ref, res_in), (dec_ref, dec_in), (skip_ref, skip_in))):
         ship.append(send(source, target, par_send.at[n], par_recv.at[n], sec_next, ctx))
     feat_copies = []
-    for j in range(tiles):
-        for part in range(3):
-            feat_copies.append(
-                send(
-                    feat_ref.at[0, :, pl.ds(part * channels + j * LANES, LANES)], fbox.at[j, part],
-                    feat_send.at[j, part], feat_recv.at[j, part], sec_next, ctx,
-                )
+    for j, part in [(j, part) for j in range(tiles) for part in (1, 2)] + [(j, 0) for j in range(tiles)]:
+        feat_copies.append(
+            send(
+                feat_ref.at[0, :, pl.ds(part * channels + j * LANES, LANES)], fbox.at[j, part],
+                feat_send.at[j, part], feat_recv.at[j, part], sec_next, ctx,
             )
+        )
     halo_copy = send(esend, halo, halo_send.at[0], halo_recv.at[0], sec_next, (ctx + 1) % n_ctx)
     for copy in ship + [halo_copy] + feat_copies:
         copy.start()
@@ -269,21 +268,20 @@
         out_hi[:, pl.ds(j * block, block)] = high
         out_lo[:, pl.ds(j * block, block)] = low
 
+    def shaped(j, part):
+        value = fbox[j, part].astype(F32)
+        wide = pl.ds(part * channels + j * LANES, LANES)
+        edge = halo[:, wide]
+        one = jnp.where(row == 0, edge[1:2], pltpu.roll(value, 1, 0))
+        two = jnp.where(row == 0, edge[0:1], jnp.where(row == 1, edge[1:2], pltpu.roll(value, 2, 0)))
+        t0, t1, t2 = [conv_in[i, :, wide] for i in range(3)]
+        return t0 * value + t1 * one + t2 * two
+
     def local_tile(j):
         cols = pl.ds(j * LANES, LANES)
-        for part in range(3):
-            feat_copies[3 * j + part].wait_recv()
-        shaped = []
-        for part in range(3):
-            value = fbox[j, part].astype(F32)
-            wide = pl.ds(part * channels + j * LANES, LANES)
-            edge = halo[:, wide]
-            one = jnp.where(row == 0, edge[1:2], pltpu.roll(value, 1, 0))
-            two = jnp.where(row == 0, edge[0:1], jnp.where(row == 1, edge[1:2], pltpu.roll(value, 2, 0)))
-            t0, t1, t2 = [conv_in[i, :, wide] for i in range(3)]
-            shaped.append(t0 * value + t1 * one + t2 * two)
-        query[:, cols] = shaped[0]
-        gated[...] = shaped[1] * shaped[2]
+        for copy in feat_copies[2 * j:2 * j + 2]:
+            copy.wait_recv()
+        gated[...] = shaped(j, 1) * shaped(j, 2)
         lam_j = lam_in[:, j * LANES:(j + 1) * LANES]
         w_j = w_in[:, j * LANES:(j + 1) * LANES]
         gain = jnp.broadcast_to(skip_in[:, cols], (CHUNKS, LANES))
@@ -350,6 +348,9 @@
     for j in range(1, tiles):
         local_tile(j)
 
+    for j in range(tiles):
+        feat_copies[2 * tiles + j].wait_recv()
+        query[:, pl.ds(j * LANES, LANES)] = shaped(j, 0)
     for j in range(tiles):
         send(hsend.at[0], p3.at[j], p3_send.at[0], p3_recv.at[j], sec_next, ctx).wait_recv()
     for j in range(tiles):

time: 23.6 us -> 22.8 us (0.966)
  Pallas kernels: 22.7 us -> 22 us
    pallas_call x1, Pallas kernels: 22.7 us -> 22 us  [on_device(): pl.pallas_call(functools.partial(kernel, n_section, n_ctx, rows, channels...]
where the time goes in v5:
time: 22.8 us; the launch traced here: 22.7 us
  Pallas kernels  22 us (96%)
  local copies, waits for them, and re-layouts  0.71 us (3%)
    pallas_call x1, Pallas kernels, on_device(): pl.pallas_call(functools.partial(kernel, n_section, n_ctx, rows, channels...  22 us
    unnamed x1, local copies, waits for them, and re-layouts  0.71 us

profile of v5, /device:TPU:2, one launch (start us, length us, event | category | flops | bytes accessed | tf_op | source)
XLA Modules:
  0.0 22.7 jit_solution(13429726769996990785)
XLA Ops:
  0.0 22.0 %mixer.1 = bf16[1,256,512]{2,1,0:T(8,128)(2,1)S(1)} custom-call(bf16[1,256,1536]{2,1,0:T(8,128)(2,1)} %feat_ref.1, f32[3,1,1536]{2,1,0:T(1,128)} %bitcast.3, f32[1,16,32]{2,1,0:T(8,128)} %bitcast.4, f32[1,16,32]{2,1,0:T(8,128)} %bitcast.5, f32[1,512]{1,0:T(1,128)} %skip_ref.1), custom_call_target="tpu_custom_call" | custom-call | tf_op jit(solution)/shard_map/mixer/pallas_call | solution.py:390
  22.0 0.7 %copy.7 = bf16[1,256,512]{2,1,0:T(8,128)(2,1)} copy(bf16[1,256,512]{2,1,0:T(8,128)(2,1)S(1)} %mixer.1) | data formatting | bytes 524288

commit v6 on v5

--- a/solution.py
+++ b/solution.py
@@ -58,7 +58,7 @@
     n_section, n_ctx, rows, channels, groups, modes,
     feat_ref, conv_ref, res_ref, dec_ref, skip_ref, out_ref,
     kv, qlast, own_lam, own_w, gate_hi, gate_lo, outbox, esend, p1, ebox, rsend, p2, acc, pre, hsend, p3,
-    fbox, halo, conv_in, res_in, dec_in, skip_in, gated, query, mixed, out_hi, out_lo,
+    fbox, halo, conv_in, res_in, dec_in, skip_in, gated, mixed, out_hi, out_lo,
     local_sem, par_send, par_recv, feat_send, feat_recv, halo_send, halo_recv,
     p1_send, p1_recv, edge_send, edge_recv, p2_send, p2_recv, p3_send, p3_recv, here,
 ):
@@ -349,17 +349,16 @@
         local_tile(j)
 
     for j in range(tiles):
-        feat_copies[2 * tiles + j].wait_recv()
-        query[:, pl.ds(j * LANES, LANES)] = shaped(j, 0)
-    for j in range(tiles):
         send(hsend.at[0], p3.at[j], p3_send.at[0], p3_recv.at[j], sec_next, ctx).wait_recv()
     for j in range(tiles):
-        cols = pl.ds(j * LANES, LANES)
         state = p3[j]
         spread = jnp.where(keep, jnp.concatenate([state] * (block // modes), axis=0), 0.0)
         wide = pl.ds(j * block, block)
         carried = dot3((out_hi[:, wide], out_lo[:, wide]), split(spread))
-        out_ref[0, :, cols] = (query[:, cols] * (mixed[j] + carried)).astype(BF16)
+        mixed[j] = mixed[j] + carried
+    for j in range(tiles):
+        feat_copies[2 * tiles + j].wait_recv()
+        out_ref[0, :, pl.ds(j * LANES, LANES)] = (shaped(j, 0) * mixed[j]).astype(BF16)
 
     for copy in ship + [halo_copy] + feat_copies + p1_copies + p3_copies:
         copy.wait_send()
@@ -416,7 +415,6 @@
             vmem(decay_rates.shape, F32),
             vmem(skip_gain.shape, F32),
             vmem((rows, LANES), F32),
-            vmem((rows, channels), F32),
             vmem((tiles, rows, LANES), F32),
             vmem((rows, groups * modes), BF16),
             vmem((rows, groups * modes), BF16),

time: 22.8 us -> 23.1 us (1.013)
  no operation moved by 1% of the time
where the time goes in v6:
time: 23.1 us; the launch traced here: 22.9 us
  Pallas kernels  22.2 us (96%)
  local copies, waits for them, and re-layouts  0.71 us (3%)
    pallas_call x1, Pallas kernels, on_device(): pl.pallas_call(functools.partial(kernel, n_section, n_ctx, rows, channels...  22.2 us
    unnamed x1, local copies, waits for them, and re-layouts  0.71 us

profile of v6, /device:TPU:2, one launch (start us, length us, event | category | flops | bytes accessed | tf_op | source)
XLA Modules:
  0.0 22.9 jit_solution(16630084198931687385)
XLA Ops:
  0.0 22.2 %mixer.1 = bf16[1,256,512]{2,1,0:T(8,128)(2,1)S(1)} custom-call(bf16[1,256,1536]{2,1,0:T(8,128)(2,1)} %feat_ref.1, f32[3,1,1536]{2,1,0:T(1,128)} %bitcast.3, f32[1,16,32]{2,1,0:T(8,128)} %bitcast.4, f32[1,16,32]{2,1,0:T(8,128)} %bitcast.5, f32[1,512]{1,0:T(1,128)} %skip_ref.1), custom_call_target="tpu_custom_call" | custom-call | tf_op jit(solution)/shard_map/mixer/pallas_call | solution.py:389
  22.2 0.7 %copy.7 = bf16[1,256,512]{2,1,0:T(8,128)(2,1)} copy(bf16[1,256,512]{2,1,0:T(8,128)(2,1)S(1)} %mixer.1) | data formatting | bytes 524288
